TPU v7x, 256 devices: a whole 4x4x8 slice. The times are simulated.
256 devices in a mesh: row: 16 (over y, x), col: 16 (over z, core).
Axes of the slice: x: 4, y: 4, z: 8, core: 2. Of those that a mesh axis runs over, the one named last changes fastest.
Arguments:
- matrix: float32 [20480, 8, 2048], P('row', None, 'col'), may hold values from -36 to 36, as said below
Outputs:
- factors: float32 [20480, 8, 2048], P('row', None, 'col')
- upper: float32 [256, 8, 2048], P(None, None, 'col')
Inputs may be any that keep to these rules, and one draw needn't show every extreme that they name: A dense real matrix of full column rank.
All inputs are finite; a program needn't handle non-finite values.
Results may differ from a plain program's by a relative error of at most 0.0003.
Values sent between devices are 32-bit elements; how exact they have to be, the bound alone decides.
No kernel may reach another device: no remote copies, remote signals or barrier semaphores. Data moves between devices by JAX's collectives and lax.ppermute only.
A program may use at most 64 MiB of HBM per device.

v0:
```python
import math
import jax
import jax.numpy as jnp
from jax import lax
from jax.sharding import PartitionSpec as P


def spread(array, axis, root):
    mine = lax.axis_index(axis) == root
    return lax.psum(jnp.where(mine, array, jnp.zeros_like(array)), axis)


def upper_factor(gram):
    size = gram.shape[0]
    places = jnp.arange(size)

    def turn(j, carry):
        rest, lower = carry
        unit = (places == j).astype(gram.dtype)
        column = jnp.sum(rest * unit[None, :], axis=1)
        pivot = jnp.sqrt(jnp.sum(column * unit))
        column = jnp.where(places >= j, column / pivot, jnp.zeros_like(column))
        rest = rest - column[:, None] * column[None, :]
        lower = lower + column[:, None] * unit[None, :]
        return (rest, lower)

    rest, lower = lax.fori_loop(0, size, turn, (gram, jnp.zeros_like(gram)))
    return lower.T


def upper_inverse(factor):
    size = factor.shape[0]
    places = jnp.arange(size)

    def turn(step, inverse):
        j = size - 1 - step
        unit = (places == j).astype(factor.dtype)
        row_vals = jnp.sum(factor * unit[:, None], axis=0)
        pivot = jnp.sum(row_vals * unit)
        new_row = (unit - jnp.sum(row_vals[:, None] * inverse, axis=0)) / pivot
        return inverse + unit[:, None] * new_row[None, :]

    return lax.fori_loop(0, size, turn, jnp.zeros_like(factor))


def orthonormal(panel_rows):
    highest = lax.Precision.HIGHEST
    gram = jnp.dot(panel_rows.T, panel_rows, precision=highest, preferred_element_type=jnp.float32)
    factor = upper_factor(lax.psum(gram, "row"))
    return jnp.dot(
        panel_rows, upper_inverse(factor), precision=highest, preferred_element_type=jnp.float32
    )


def basis_for(block, spare, owner):
    source = jnp.where(lax.axis_index("col") == owner, block, spare)
    return spread(orthonormal(source), "col", owner)


def project(basis, work):
    local = jnp.einsum(
        "rp,rbc->pbc",
        basis,
        work,
        precision=lax.Precision.HIGHEST,
        preferred_element_type=jnp.float32,
    )
    return lax.psum(local, "row")


def remove(work, basis, coeffs):
    return work - jnp.einsum(
        "rp,pbc->rbc",
        basis,
        coeffs,
        precision=lax.Precision.HIGHEST,
        preferred_element_type=jnp.float32,
    )


def shards(matrix):
    scale = math.sqrt(matrix.shape[0] * lax.axis_size("row"))
    spare = matrix[:, 0, :]
    first = basis_for(matrix[:, 0, :], spare, 0)
    coef_one = project(first, matrix)
    middle = remove(matrix, first, coef_one)
    second = basis_for(middle[:, 0, :], spare, 1)
    coef_two = project(second, middle)
    final = remove(middle, second, coef_two)
    column = lax.axis_index("col")
    lead_block = jnp.where(
        column == 0, first * scale, jnp.where(column == 1, second * scale, final[:, 0, :])
    )
    factors = jnp.concatenate([lead_block[:, None, :], final[:, 1:, :]], axis=1)
    upper = jnp.concatenate([coef_one, coef_two], axis=0) / scale
    return (factors, upper)


def solution(mesh):
    in_specs = (P("row", None, "col"),)
    out_specs = (P("row", None, "col"), P(None, None, "col"))
    return jax.shard_map(shards, mesh=mesh, in_specs=in_specs, out_specs=out_specs, check_vma=False)
```

profile of v0, /device:TPU:32, one launch (start us, length us, event | category | flops | bytes accessed | tf_op | source)
XLA Modules:
  0.0 2057.3 jit_solution(17769544021011634935)
XLA Ops:
  7.2 6.2 copy.3
  13.4 2.6 fusion.26
  16.1 93.7 %all-reduce.7.cloned.1.call-done = f32[128,128]{1,0:T(8,128)} async-done(((f32[128,128]{1,0:T(8,128)}), f32[128,128]{1,0:T(8,128)}) %all-reduce.7.cloned.1.call-update) | async-done | bytes 65552 | tf_op jit(solution)/shard_map/psum | solution.py:49
  109.9 488.9 %while.64 = (s32[]{:T(128)}, f32[128,128]{1,0:T(8,128)}, f32[128,128]{1,0:T(8,128)S(1)}, s32[]{:T(128)}, s32[]{:T(128)}) while((s32[]{:T(128)}, f32[128,128]{1,0:T(8,128)}, f32[128,128]{1,0:T(8,128)S(1)}, s32[]{:T(128)}, s32[]{:T(128)}) %tuple.132), condition=%wide.region_4.5_spmd.clone.clone, body=%wide.region_1.4_spmd.clone.clone.sunk | while | flops 115586 | bytes 331883 | solution.py:27
  598.8 203.2 %while.62 = (s32[]{:T(128)}, f32[128,128]{1,0:T(8,128)S(1)}, f32[128,128]{1,0:T(8,128)S(1)}, s32[]{:T(128)}, s32[]{:T(128)}, /*index=5*/s32[]{:T(128)}) while((s32[]{:T(128)}, f32[128,128]{1,0:T(8,128)S(1)}, f32[128,128]{1,0:T(8,128)S(1)}, s32[]{:T(128)}, s32[]{:T(128)}, /*index=5*/s32[]{:T(128)}) %tuple.135), condition=%wide.region_9.10_spmd.clone, body=%wide.region_5.9_spmd.clone.sunk | while | flops 131971 | bytes 267384 | solution.py:43
  802.1 2.6 fusion.12
  804.8 107.2 %all-reduce.9.cloned.1.call-done = f32[1280,128]{0,1:T(8,128)} async-done(((f32[1280,128]{0,1:T(8,128)}), f32[1280,128]{0,1:T(8,128)}) %all-reduce.9.cloned.1.call-update) | async-done | bytes 655376 | tf_op jit(solution)/shard_map/psum | solution.py:10
  912.0 8.9 fusion.21
  921.0 98.3 %all-reduce.11.cloned.1.call-done = f32[128,8,128]{2,0,1:T(8,128)} async-done(((f32[128,8,128]{2,0,1:T(8,128)}), f32[128,8,128]{2,0,1:T(8,128)}) %all-reduce.11.cloned.1.call-update) | async-done | bytes 524304 | tf_op jit(solution)/shard_map/psum | solution.py:68
  1019.3 7.4 convolution_subtract_fusion.1
  1026.7 2.3 copy-done
  1029.0 2.6 fusion.19
  1032.0 90.3 %all-reduce.13.cloned.1.call-done = f32[128,128]{1,0:T(8,128)} async-done(((f32[128,128]{1,0:T(8,128)}), f32[128,128]{1,0:T(8,128)}) %all-reduce.13.cloned.1.call-update) | async-done | bytes 65552 | tf_op jit(solution)/shard_map/psum | solution.py:49
  1122.3 489.1 %while.65 = (s32[]{:T(128)}, f32[128,128]{1,0:T(8,128)}, f32[128,128]{1,0:T(8,128)S(1)}, s32[]{:T(128)}, s32[]{:T(128)}) while((s32[]{:T(128)}, f32[128,128]{1,0:T(8,128)}, f32[128,128]{1,0:T(8,128)S(1)}, s32[]{:T(128)}, s32[]{:T(128)}) %tuple.138), condition=%wide.region_16.17_spmd.clone.clone, body=%wide.region_13.16_spmd.clone.clone.sunk | while | flops 115586 | bytes 331883 | solution.py:27
  1124.6 1.6 select_add_fusion.5
  1128.4 1.6 select_add_fusion.5
  1132.2 1.6 select_add_fusion.5
  1136.0 1.6 select_add_fusion.5
  1139.8 1.6 select_add_fusion.5
  1143.7 1.6 select_add_fusion.5
  1147.5 1.6 select_add_fusion.5
  1151.3 1.6 select_add_fusion.5
  1155.1 1.6 select_add_fusion.5
  1158.9 1.6 select_add_fusion.5
  1162.8 1.6 select_add_fusion.5
  1166.6 1.6 select_add_fusion.5
  1170.4 1.6 select_add_fusion.5
  1174.2 1.6 select_add_fusion.5
  1178.0 1.6 select_add_fusion.5
  1181.9 1.6 select_add_fusion.5
  1185.7 1.6 select_add_fusion.5
  1189.5 1.6 select_add_fusion.5
  1201.0 1.6 select_add_fusion.5
  1231.5 1.6 select_add_fusion.5
  1243.0 1.6 select_add_fusion.5
  1262.1 1.6 select_add_fusion.5
  1273.6 1.6 select_add_fusion.5
  1304.1 1.6 select_add_fusion.5
  1315.6 1.6 select_add_fusion.5
  1334.7 1.6 select_add_fusion.5
  1346.2 1.6 select_add_fusion.5
  1376.7 1.6 select_add_fusion.5
  1388.2 1.6 select_add_fusion.5
  1407.3 1.6 select_add_fusion.5
  1418.8 1.6 select_add_fusion.5
  1449.3 1.6 select_add_fusion.5
  1460.8 1.6 select_add_fusion.5
  1479.9 1.6 select_add_fusion.5
  1491.4 1.6 select_add_fusion.5
  1521.9 1.6 select_add_fusion.5
  1533.4 1.6 select_add_fusion.5
  1552.5 1.6 select_add_fusion.5
  1564.0 1.6 select_add_fusion.5
  1594.5 1.6 select_add_fusion.5
  1606.0 1.6 select_add_fusion.5
  1611.5 203.2 %while.63 = (s32[]{:T(128)}, f32[128,128]{1,0:T(8,128)S(1)}, f32[128,128]{1,0:T(8,128)S(1)}, s32[]{:T(128)}, s32[]{:T(128)}, /*index=5*/s32[]{:T(128)}) while((s32[]{:T(128)}, f32[128,128]{1,0:T(8,128)S(1)}, f32[128,128]{1,0:T(8,128)S(1)}, s32[]{:T(128)}, s32[]{:T(128)}, /*index=5*/s32[]{:T(128)}) %tuple.141), condition=%wide.region_21.22_spmd.clone, body=%wide.region_17.21_spmd.clone.sunk | while | flops 131971 | bytes 267384 | solution.py:43
  1814.7 2.9 convolution_select_fusion
  1817.7 107.2 %all-reduce.15.cloned.1.call-done = f32[1280,128]{0,1:T(8,128)} async-done(((f32[1280,128]{0,1:T(8,128)}), f32[1280,128]{0,1:T(8,128)}) %all-reduce.15.cloned.1.call-update) | async-done | bytes 655376 | tf_op jit(solution)/shard_map/psum | solution.py:10
  1924.8 8.9 fusion.16
  1933.8 98.4 %all-reduce.17.cloned.1.call-done = f32[128,8,128]{2,0,1:T(8,128)} async-done(((f32[128,8,128]{2,0,1:T(8,128)}), f32[128,8,128]{2,0,1:T(8,128)}) %all-reduce.17.cloned.1.call-update) | async-done | bytes 524304 | tf_op jit(solution)/shard_map/psum | solution.py:68
  2032.2 7.0 convolution_subtract_fusion
  2039.7 2.7 pad_maximum_fusion
  2042.4 6.3 copy.14
  2048.9 1.6 copy.15
  (2805 shorter events, 1130.3 us)
Async XLA Ops:
  7.2 102.7 %all-reduce.7.cloned.1.call-start = ((), (), s32[]{:S(2)}) async-start(), calls=%async_computation | async-start | bytes 131072 | tf_op jit(solution)/shard_map/psum | solution.py:49
  16.1 895.9 %all-reduce.9.cloned.1.call-start = ((), (), s32[]{:S(2)}) async-start(), calls=%async_computation.1 | async-start | bytes 1310720 | tf_op jit(solution)/shard_map/psum | solution.py:10
  804.8 214.6 %all-reduce.11.cloned.1.call-start = ((), (), s32[]{:S(2)}) async-start(), calls=%async_computation.2 | async-start | bytes 1048576 | tf_op jit(solution)/shard_map/psum | solution.py:68
  912.0 107.3 %copy-start.1 = (f32[1280,128]{0,1:T(8,128)S(1)}, f32[1280,128]{0,1:T(8,128)}, u32[]{:S(2)}) copy-start(f32[1280,128]{0,1:T(8,128)} %all-reduce.9.cloned.1.call-done) | copy-start | bytes 1966084
  921.0 201.3 %all-reduce.13.cloned.1.call-start = ((), (), s32[]{:S(2)}) async-start(), calls=%async_computation.3 | async-start | bytes 131072 | tf_op jit(solution)/shard_map/psum | solution.py:49
  1026.7 2.3 copy-start
  1031.7 893.1 %all-reduce.15.cloned.1.call-start = ((), (), s32[]{:S(2)}) async-start(), calls=%async_computation.4 | async-start | bytes 1310720 | tf_op jit(solution)/shard_map/psum | solution.py:10
  1817.6 214.6 %all-reduce.17.cloned.1.call-start = ((), (), s32[]{:S(2)}) async-start(), calls=%async_computation.5 | async-start | bytes 1048576 | tf_op jit(solution)/shard_map/psum | solution.py:68
  1924.8 107.3 %copy-start.2 = (f32[1280,128]{0,1:T(8,128)S(1)}, f32[1280,128]{0,1:T(8,128)}, u32[]{:S(2)}) copy-start(f32[1280,128]{0,1:T(8,128)} %all-reduce.15.cloned.1.call-done) | copy-start | bytes 1966084
  2042.4 6.3 copy-start.3
  2042.4 6.3 copy-start.4
Sparse Core Ops, SparseCore 0:
  16.2 93.6 all-reduce.6
  804.9 107.0 all-reduce.8
  921.1 98.1 all-reduce.10
  1031.8 90.4 all-reduce.12
  1817.7 107.0 all-reduce.14
  1933.9 98.2 all-reduce.16
where the time goes:
time: 2090 us; the launch traced here: 2060 us
  other arithmetic  1200 us (57%)
  waiting for transfers between devices  595 us (28%)
  loops' own time  192 us (9%)
  matrix products  43 us (2%)
    add x256, other arithmetic, turn(): lower = lower + column[:, None] * unit[None, :]  398 us
    reduce_sum x256, other arithmetic, turn(): column = jnp.sum(rest * unit[None, :], axis=1)  241 us
    psum x2, waiting for transfers between devices, spread(): return lax.psum(jnp.where(mine, array, jnp.zeros_like(array)), axis)  214 us
    psum x2, waiting for transfers between devices, project(): return lax.psum(local, 'row')  197 us
    psum x2, waiting for transfers between devices, orthonormal(): factor = upper_factor(lax.psum(gram, 'row'))  184 us
    another operation x2, loops' own time, upper_factor(): rest, lower = lax.fori_loop(0, size, turn, (gram, jnp.zeros_like(gram)))  181 us
    div x256, other arithmetic, turn(): new_row = (unit - jnp.sum(row_vals[:, None] * inverse, axis=0)) / pivot  168 us
    reduce_sum x256, other arithmetic, turn(): pivot = jnp.sqrt(jnp.sum(column * unit))  157 us
  transfers between devices with their start and end apart: 6, of which 6 were waited for; matrix products, arithmetic and copies ran while one was open for 0% of the time, Pallas kernels for 0%

commit v1 on v0

--- a/solution.py
+++ b/solution.py
@@ -7,7 +7,7 @@
 
 def spread(array, axis, root):
     mine = lax.axis_index(axis) == root
-    return lax.psum(jnp.where(mine, array, jnp.zeros_like(array)), axis)
+    return jnp.sum(lax.all_gather(jnp.where(mine, array, jnp.zeros_like(array)), axis), axis=0)
 
 
 def upper_factor(gram):

time: 2090 us -> 2010 us (0.962)
  waiting for transfers between devices: 595 us -> 502 us
    psum x2 -> x0, waiting for transfers between devices: 214 us -> none  [spread(): return lax.psum(jnp.where(mine, array, jnp.zeros_like(array)), axis)]
    all_gather x0 -> x2, waiting for transfers between devices: none -> 127 us  [spread(): lax.all_gather(jnp.where(mine, array, jnp.zeros_like(array)), axis)]
where the time goes in v1:
time: 2010 us; the launch traced here: 1980 us
  other arithmetic  1200 us (60%)
  waiting for transfers between devices  502 us (25%)
  loops' own time  193 us (10%)
  matrix products  35.3 us (2%)
  local copies, waits for them, and re-layouts  30 us (1%)
    add x256, other arithmetic, turn(): lower = lower + column[:, None] * unit[None, :]  397 us
    reduce_sum x256, other arithmetic, turn(): column = jnp.sum(rest * unit[None, :], axis=1)  241 us
    psum x2, waiting for transfers between devices, project(): return lax.psum(local, 'row')  191 us
    psum x2, waiting for transfers between devices, orthonormal(): factor = upper_factor(lax.psum(gram, 'row'))  184 us
    another operation x2, loops' own time, upper_factor(): rest, lower = lax.fori_loop(0, size, turn, (gram, jnp.zeros_like(gram)))  182 us
    div x256, other arithmetic, turn(): new_row = (unit - jnp.sum(row_vals[:, None] * inverse, axis=0)) / pivot  168 us
    reduce_sum x256, other arithmetic, turn(): pivot = jnp.sqrt(jnp.sum(column * unit))  157 us
    reduce_sum x256, other arithmetic, turn(): pivot = jnp.sum(row_vals * unit)  156 us
  transfers between devices with their start and end apart: 6, of which 6 were waited for; matrix products, arithmetic and copies ran while one was open for 0% of the time, Pallas kernels for 0%

profile of v1, /device:TPU:32, one launch (start us, length us, event | category | flops | bytes accessed | tf_op | source)
XLA Modules:
  0.0 1978.2 jit_solution(2242054834089538467)
XLA Ops:
  7.2 3.5 copy.12
  10.7 2.3 copy-done.1
  13.1 1.9 fusion.24
  15.1 93.7 %all-reduce.5.cloned.1.call-done = f32[128,128]{1,0:T(8,128)} async-done(((f32[128,128]{1,0:T(8,128)}), f32[128,128]{1,0:T(8,128)}) %all-reduce.5.cloned.1.call-update) | async-done | bytes 65552 | tf_op jit(solution)/shard_map/psum | solution.py:49
  108.8 489.4 %while.64 = (s32[]{:T(128)}, f32[128,128]{1,0:T(8,128)}, f32[128,128]{1,0:T(8,128)S(1)}, s32[]{:T(128)}, s32[]{:T(128)}) while((s32[]{:T(128)}, f32[128,128]{1,0:T(8,128)}, f32[128,128]{1,0:T(8,128)S(1)}, s32[]{:T(128)}, s32[]{:T(128)}) %tuple.135), condition=%wide.region_4.5_spmd.clone.clone, body=%wide.region_1.4_spmd.clone.clone.sunk | while | flops 115586 | bytes 331875 | solution.py:27
  111.0 1.6 select_add_fusion.4
  114.9 1.6 select_add_fusion.4
  118.7 1.6 select_add_fusion.4
  122.5 1.6 select_add_fusion.4
  126.3 1.6 select_add_fusion.4
  130.2 1.6 select_add_fusion.4
  134.0 1.6 select_add_fusion.4
  137.8 1.6 select_add_fusion.4
  141.6 1.6 select_add_fusion.4
  145.5 1.6 select_add_fusion.4
  149.3 1.6 select_add_fusion.4
  153.1 1.6 select_add_fusion.4
  156.9 1.6 select_add_fusion.4
  160.7 1.6 select_add_fusion.4
  164.6 1.6 select_add_fusion.4
  168.4 1.6 select_add_fusion.4
  172.2 1.6 select_add_fusion.4
  176.0 1.6 select_add_fusion.4
  183.7 1.6 select_add_fusion.4
  187.5 1.6 select_add_fusion.4
  191.3 1.6 select_add_fusion.4
  195.2 1.6 select_add_fusion.4
  199.0 1.6 select_add_fusion.4
  202.8 1.6 select_add_fusion.4
  206.6 1.6 select_add_fusion.4
  210.5 1.6 select_add_fusion.4
  214.3 1.6 select_add_fusion.4
  218.1 1.6 select_add_fusion.4
  221.9 1.6 select_add_fusion.4
  225.8 1.6 select_add_fusion.4
  229.6 1.6 select_add_fusion.4
  233.4 1.6 select_add_fusion.4
  237.2 1.6 select_add_fusion.4
  241.0 1.6 select_add_fusion.4
  244.9 1.6 select_add_fusion.4
  248.7 1.6 select_add_fusion.4
  256.3 1.6 select_add_fusion.4
  260.2 1.6 select_add_fusion.4
  598.3 203.0 %while.62 = (s32[]{:T(128)}, f32[128,128]{1,0:T(8,128)S(1)}, f32[128,128]{1,0:T(8,128)S(1)}, s32[]{:T(128)}, s32[]{:T(128)}, /*index=5*/s32[]{:T(128)}) while((s32[]{:T(128)}, f32[128,128]{1,0:T(8,128)S(1)}, f32[128,128]{1,0:T(8,128)S(1)}, s32[]{:T(128)}, s32[]{:T(128)}, /*index=5*/s32[]{:T(128)}) %tuple.138), condition=%wide.region_9.10_spmd.clone, body=%wide.region_5.9_spmd.clone.sunk | while | flops 131971 | bytes 267376 | solution.py:43
  801.3 2.7 fusion.12
  804.2 63.3 %all-gather.5.cloned.1.call-done = f32[20480,128]{0,1:T(8,128)} async-done(((f32[1280,128]{0,1:T(8,128)}), f32[20480,128]{0,1:T(8,128)}) %all-gather.5.cloned.1.call-update) | async-done | bytes 10485776 | tf_op jit(solution)/shard_map/all_gather | solution.py:10
  867.5 11.2 copy.26
  878.7 5.8 bitcast_reduce_fusion
  884.6 4.5 fusion.19
  889.4 95.6 %all-reduce.7.cloned.1.call-done = f32[128,8,128]{2,0,1:T(8,128)} async-done(((f32[128,8,128]{2,0,1:T(8,128)}), f32[128,8,128]{2,0,1:T(8,128)}) %all-reduce.7.cloned.1.call-update) | async-done | bytes 524304 | tf_op jit(solution)/shard_map/psum | solution.py:68
  984.9 7.7 convolution_subtract_fusion.1
  992.7 2.4 copy-done
  995.0 3.2 fusion.17
  998.3 90.5 %all-reduce.9.cloned.1.call-done = f32[128,128]{1,0:T(8,128)} async-done(((f32[128,128]{1,0:T(8,128)}), f32[128,128]{1,0:T(8,128)}) %all-reduce.9.cloned.1.call-update) | async-done | bytes 65552 | tf_op jit(solution)/shard_map/psum | solution.py:49
  1088.8 489.4 %while.65 = (s32[]{:T(128)}, f32[128,128]{1,0:T(8,128)}, f32[128,128]{1,0:T(8,128)S(1)}, s32[]{:T(128)}, s32[]{:T(128)}) while((s32[]{:T(128)}, f32[128,128]{1,0:T(8,128)}, f32[128,128]{1,0:T(8,128)S(1)}, s32[]{:T(128)}, s32[]{:T(128)}) %tuple.141), condition=%wide.region_16.17_spmd.clone.clone, body=%wide.region_13.16_spmd.clone.clone.sunk | while | flops 115586 | bytes 331875 | solution.py:27
  1578.3 203.0 %while.63 = (s32[]{:T(128)}, f32[128,128]{1,0:T(8,128)S(1)}, f32[128,128]{1,0:T(8,128)S(1)}, s32[]{:T(128)}, s32[]{:T(128)}, /*index=5*/s32[]{:T(128)}) while((s32[]{:T(128)}, f32[128,128]{1,0:T(8,128)S(1)}, f32[128,128]{1,0:T(8,128)S(1)}, s32[]{:T(128)}, s32[]{:T(128)}, /*index=5*/s32[]{:T(128)}) %tuple.144), condition=%wide.region_21.22_spmd.clone, body=%wide.region_17.21_spmd.clone.sunk | while | flops 131971 | bytes 267376 | solution.py:43
  1781.3 2.8 convolution_select_fusion
  1784.2 63.5 %all-gather.7.cloned.1.call-done = f32[20480,128]{1,0:T(8,128)} async-done(((f32[1280,128]{1,0:T(8,128)}), f32[20480,128]{1,0:T(8,128)}) %all-gather.7.cloned.1.call-update) | async-done | bytes 10485776 | tf_op jit(solution)/shard_map/all_gather | solution.py:10
  1847.7 4.5 reduce_sum.149
  1852.2 6.2 fusion.14
  1858.7 95.6 %all-reduce.11.cloned.1.call-done = f32[128,8,128]{2,0,1:T(8,128)} async-done(((f32[128,8,128]{2,0,1:T(8,128)}), f32[128,8,128]{2,0,1:T(8,128)}) %all-reduce.11.cloned.1.call-update) | async-done | bytes 524304 | tf_op jit(solution)/shard_map/psum | solution.py:68
  1954.3 6.3 convolution_subtract_fusion
  1961.4 8.3 copy.20
  1969.8 1.6 copy.21
  (2812 shorter events, 1135.2 us)
Async XLA Ops:
  7.2 101.6 %all-reduce.5.cloned.1.call-start = ((), (), s32[]{:S(2)}) async-start(), calls=%async_computation | async-start | bytes 131072 | tf_op jit(solution)/shard_map/psum | solution.py:49
  10.7 2.4 copy-start.1
  15.0 852.5 %all-gather.5.cloned.1.call-start = ((), (), s32[]{:S(2)}) async-start(), calls=%async_computation.4 | async-start | bytes 11141120 | tf_op jit(solution)/shard_map/all_gather | solution.py:10
  803.9 80.6 %slice-start = ((s8[5242880]{0:T(1024)(128)(4,1)}), s8[1048576]{0:T(1024)(128)(4,1)S(1)}, s32[]{:S(2)}) async-start(s8[5242880]{0:T(1024)(128)(4,1)} %bitcast.46), calls=%async_computation.6 | async-start | bytes 2097152
  804.0 180.9 %all-reduce.7.cloned.1.call-start = ((), (), s32[]{:S(2)}) async-start(), calls=%async_computation.1 | async-start | bytes 1048576 | tf_op jit(solution)/shard_map/psum | solution.py:68
  867.5 17.0 slice-start.1
  889.1 199.7 %all-reduce.9.cloned.1.call-start = ((), (), s32[]{:S(2)}) async-start(), calls=%async_computation.2 | async-start | bytes 131072 | tf_op jit(solution)/shard_map/psum | solution.py:49
  992.7 2.4 copy-start
  998.2 849.4 %all-gather.7.cloned.1.call-start = ((), (), s32[]{:S(2)}) async-start(), calls=%async_computation.5 | async-start | bytes 11141120 | tf_op jit(solution)/shard_map/all_gather | solution.py:10
  1784.1 170.1 %all-reduce.11.cloned.1.call-start = ((), (), s32[]{:S(2)}) async-start(), calls=%async_computation.3 | async-start | bytes 1048576 | tf_op jit(solution)/shard_map/psum | solution.py:68
  1961.4 8.3 copy-start.2
  1961.4 8.3 copy-start.3
Sparse Core Ops, SparseCore 0:
  15.1 93.6 all-reduce.4
  804.1 63.3 all-gather.4
  889.2 95.6 all-reduce.6
  998.4 90.4 all-reduce.8
  1784.3 63.3 all-gather.6
  1858.6 95.6 all-reduce.10
